TPU v7x, 32 devices: a whole 2x2x4 slice. The times are simulated.
32 devices in a mesh: dp: 4 (over z), expert: 8 (over y, x, core).
Axes of the slice: x: 2, y: 2, z: 4, core: 2. Of those that a mesh axis runs over, the one named last changes fastest.
Arguments:
- tokens: bfloat16 [8192, 1536], P(('dp', 'expert')), may hold values from -6 to 6
- segment_ids: int32 [8192], P('dp'), may hold values from 0 to 7, never falling along the last dimension, each value on 1 to 2048 neighbouring positions
- expert_ids: int32 [8192, 8], P(('dp', 'expert')), may hold values from 0 to 15, all different within a row; in each aligned block of 256 rows (0 to 255, 256 to 511, ...) at most 160 rows name the same one
- w_query: bfloat16 [1536, 1536], P(('dp', 'expert')), may hold values from -0.5 to 0.5
- w_key_value: bfloat16 [1536, 1024], P(('dp', 'expert')), may hold values from -0.5 to 0.5
- w_out: bfloat16 [1536, 1536], P(None, ('dp', 'expert')), may hold values from -1.75 to 1.75
- w_router: bfloat16 [1536, 16], P(('dp', 'expert')), may hold values from -0.078125 to 0.078125
- norm_attn: bfloat16 [1536], P(('dp', 'expert')), may hold values from 0.5 to 1.5
- norm_moe: bfloat16 [1536], P(('dp', 'expert')), may hold values from 0.5 to 1.5
- w_gate_up: bfloat16 [16, 1536, 1024], P('expert'), may hold values from -0.15625 to 0.15625
- w_down: bfloat16 [16, 512, 1536], P('expert'), may hold values from -6 to 6
- grad_out: bfloat16 [8192, 1536], P(('dp', 'expert')), may hold values from -6 to 6
Outputs:
- result: bfloat16 [8192, 1536], P(('dp', 'expert'))
- grad_tokens: bfloat16 [8192, 1536], P(('dp', 'expert'))
- grad_w_query: float32 [1536, 1536], P(('dp', 'expert'))
- grad_w_key_value: float32 [1536, 1024], P(('dp', 'expert'))
- grad_w_out: float32 [1536, 1536], P(None, ('dp', 'expert'))
- grad_w_router: float32 [1536, 16], P(('dp', 'expert'))
- grad_norm_attn: float32 [1536], P(('dp', 'expert'))
- grad_norm_moe: float32 [1536], P(('dp', 'expert'))
- grad_w_gate_up: float32 [16, 1536, 1024], P('expert', 'dp')
- grad_w_down: float32 [16, 512, 1536], P('expert', None, 'dp')
Inputs may be any that keep to these rules, and one draw needn't show every extreme that they name: `expert_ids`: within the 256 tokens of one device a row names 8 different experts, and no expert is named more than 160 times; in every draw some expert is named exactly 160 times by one device's tokens.
All inputs are finite; a program needn't handle non-finite values.
Results may differ from a plain program's by a relative error of at most 0.02.
Values may be sent and summed in bfloat16 or wider, within the bound.
No kernel may reach another device: no remote copies, remote signals or barrier semaphores. Data moves between devices by JAX's collectives and lax.ppermute only.
A program may use at most 256 MiB of HBM per device.

v0:
```python
import jax
import jax.numpy as jnp
from jax import lax
from jax.sharding import PartitionSpec as P

D = 1536
HEADS = 24
KV_HEADS = 8
HEAD_DIM = 64
FF = 512
TOP = 8
EXP_DEV = 2
SEQ_MIN = 1024
RESIDUAL = 0.22
ATTN_SCALE = 0.015625
EPSILON = 1e-06
ROPE_BASE = 10000.0
MASKED = -1e30


def rms_scale(values, gain_vec):
    return (
        values * lax.rsqrt(jnp.mean(values * values, axis=-1, keepdims=True) + EPSILON) * gain_vec
    )


def rope_tables(position):
    half_dim = HEAD_DIM // 2
    frequency = ROPE_BASE ** (-(jnp.arange(half_dim, dtype=jnp.float32) * 2.0 / HEAD_DIM))
    angles = position.astype(jnp.float32)[:, None] * frequency[None, :]
    return (jnp.cos(angles), jnp.sin(angles))


def rotate(flat_rows, cosine, sine_table):
    row_count = flat_rows.shape[0]
    pieces = flat_rows.reshape(row_count, -1, HEAD_DIM)
    half_dim = HEAD_DIM // 2
    first_half = pieces[..., :half_dim]
    second_half = pieces[..., half_dim:]
    cos_part = cosine[:, None, :]
    sin_part = sine_table[:, None, :]
    turned = jnp.concatenate(
        [
            first_half * cos_part - second_half * sin_part,
            second_half * cos_part + first_half * sin_part,
        ],
        axis=-1,
    )
    return turned.reshape(row_count, -1)


def slot_index(route_flat, expert_total, capacity):
    one_hot = (route_flat[:, None] == jnp.arange(expert_total, dtype=jnp.int32)).astype(jnp.int32)
    rank_table = jnp.cumsum(one_hot, axis=0) - 1
    slot_number = jnp.sum(rank_table * one_hot, axis=-1)
    return route_flat * capacity + slot_number


def split_heads(pair_rows):
    pair_width = KV_HEADS * HEAD_DIM
    key_heads = jnp.moveaxis(pair_rows[:, :pair_width].reshape(-1, KV_HEADS, HEAD_DIM), 1, 0)
    value_heads = jnp.moveaxis(pair_rows[:, pair_width:].reshape(-1, KV_HEADS, HEAD_DIM), 1, 0)
    return (key_heads, value_heads)


def shards(
    tokens,
    segment_ids,
    expert_ids,
    w_query,
    w_key_value,
    w_out,
    w_router,
    norm_attn,
    norm_moe,
    w_gate_up,
    w_down,
    grad_out,
):
    full_query, full_pair, full_out, full_router, gain_attn, gain_moe = (
        lax.all_gather(w_query, ("dp", "expert"), axis=0, tiled=True),
        lax.all_gather(w_key_value, ("dp", "expert"), axis=0, tiled=True),
        lax.all_gather(w_out, ("dp", "expert"), axis=1, tiled=True),
        lax.all_gather(w_router, ("dp", "expert"), axis=0, tiled=True),
        lax.all_gather(norm_attn, ("dp", "expert"), axis=0, tiled=True),
        lax.all_gather(norm_moe, ("dp", "expert"), axis=0, tiled=True),
    )
    gain_attn = gain_attn.astype(jnp.float32)
    gain_moe = gain_moe.astype(jnp.float32)
    tok_rows = tokens.shape[0]
    members = lax.axis_size("expert")
    position = lax.axis_index("expert")
    seq_length = max(SEQ_MIN, tok_rows * members)
    expert_total = EXP_DEV * members
    capacity = min(tok_rows, 5 * tok_rows * TOP // (4 * expert_total))
    pair_width = KV_HEADS * HEAD_DIM
    group_size = HEADS // KV_HEADS
    query_pos = position * tok_rows + jnp.arange(tok_rows, dtype=jnp.int32)
    key_start = position * tok_rows // seq_length * seq_length
    key_pos = key_start + jnp.arange(seq_length, dtype=jnp.int32)
    query_seg = lax.dynamic_slice_in_dim(segment_ids, position * tok_rows, tok_rows, 0)
    allowed = (query_seg[:, None] == segment_ids[None, :]) & (
        query_pos[:, None] >= key_pos[None, :]
    )
    cosine, sine_table = rope_tables(query_pos % seq_length)
    tokens_f = tokens.astype(jnp.float32)
    normed = rms_scale(tokens_f, gain_attn).astype(jnp.bfloat16)
    queries = jnp.dot(normed, full_query, preferred_element_type=jnp.float32)
    key_value = jnp.dot(normed, full_pair, preferred_element_type=jnp.float32)
    queries_low = rotate(queries, cosine, sine_table).astype(jnp.bfloat16)
    pair_low = jnp.concatenate(
        [rotate(key_value[:, :pair_width], cosine, sine_table), key_value[:, pair_width:]], axis=1
    ).astype(jnp.bfloat16)
    pair_group = lax.all_gather(pair_low, "expert", axis=0, tiled=True)
    query_heads = jnp.moveaxis(queries_low.reshape(tok_rows, KV_HEADS, group_size, HEAD_DIM), 1, 0)
    key_heads, value_heads = split_heads(pair_group)

    def head_probs(query_head, key_head):
        raw_scores = jnp.einsum(
            "qgd,kd->gqk", query_head, key_head, preferred_element_type=jnp.float32
        )
        scores = jnp.where(allowed[None], raw_scores * ATTN_SCALE, MASKED)
        largest = jnp.max(scores, axis=-1, keepdims=True)
        exponent = jnp.exp(scores - largest)
        return exponent / jnp.sum(exponent, axis=-1, keepdims=True)

    def head_forward(operands):
        query_head, key_head, value_head = operands
        probability = head_probs(query_head, key_head)
        return jnp.einsum(
            "gqk,kd->qgd",
            probability.astype(jnp.bfloat16),
            value_head,
            preferred_element_type=jnp.float32,
        )

    attended = lax.map(head_forward, (query_heads, key_heads, value_heads))
    mixed_low = (
        jnp.moveaxis(attended, 0, 1).reshape(tok_rows, HEADS * HEAD_DIM).astype(jnp.bfloat16)
    )
    after_attn = tokens_f + RESIDUAL * jnp.dot(
        mixed_low, full_out, preferred_element_type=jnp.float32
    )
    normed_moe = rms_scale(after_attn, gain_moe).astype(jnp.bfloat16)
    logits = jnp.dot(normed_moe, full_router, preferred_element_type=jnp.float32)
    one_hot = (expert_ids[:, :, None] == jnp.arange(expert_total, dtype=jnp.int32)).astype(
        jnp.float32
    )
    chosen = jnp.sum(one_hot * logits[:, None, :], axis=-1)
    gate_weights = jax.nn.softmax(chosen, axis=-1)
    targets = slot_index(expert_ids.reshape(-1), expert_total, capacity)
    routed = jnp.repeat(normed_moe, TOP, axis=0)
    send_rows = (
        jnp.zeros((expert_total * capacity, D), jnp.bfloat16)
        .at[targets]
        .set(routed)
        .reshape(members, EXP_DEV * capacity, D)
    )
    arrived = lax.all_to_all(send_rows, "expert", split_axis=0, concat_axis=0, tiled=True).reshape(
        members, EXP_DEV, capacity, D
    )
    gate_up = jnp.einsum("secd,edf->secf", arrived, w_gate_up, preferred_element_type=jnp.float32)
    gate_part = gate_up[..., :FF]
    up_part = gate_up[..., FF:]
    activated = (jax.nn.silu(gate_part) * up_part).astype(jnp.bfloat16)
    expert_out = jnp.einsum(
        "secf,efd->secd", activated, w_down, preferred_element_type=jnp.float32
    ).astype(jnp.bfloat16)
    replies = lax.all_to_all(
        expert_out.reshape(members, EXP_DEV * capacity, D),
        "expert",
        split_axis=0,
        concat_axis=0,
        tiled=True,
    ).reshape(expert_total * capacity, D)
    returned_f = replies[targets].reshape(tok_rows, TOP, D).astype(jnp.float32)
    combined = jnp.sum(gate_weights[:, :, None] * returned_f, axis=1)
    result = (after_attn + RESIDUAL * combined).astype(jnp.bfloat16)
    grad_final = grad_out.astype(jnp.float32)
    gate_grads = RESIDUAL * jnp.sum(returned_f * grad_final[:, None, :], axis=-1)
    out_grads = (
        (gate_weights[:, :, None] * (RESIDUAL * grad_final)[:, None, :])
        .astype(jnp.bfloat16)
        .reshape(tok_rows * TOP, D)
    )
    send_grads = (
        jnp.zeros((expert_total * capacity, D), jnp.bfloat16)
        .at[targets]
        .set(out_grads)
        .reshape(members, EXP_DEV * capacity, D)
    )
    arrived_grads = lax.all_to_all(
        send_grads, "expert", split_axis=0, concat_axis=0, tiled=True
    ).reshape(members, EXP_DEV, capacity, D)
    act_grads = jnp.einsum(
        "secd,efd->secf", arrived_grads, w_down, preferred_element_type=jnp.float32
    )
    down_wgrads = jnp.einsum(
        "secf,secd->efd", activated, arrived_grads, preferred_element_type=jnp.float32
    )
    sigmoid_gate = jax.nn.sigmoid(gate_part)
    grad_gate = act_grads * up_part * sigmoid_gate * (1.0 + gate_part * (1.0 - sigmoid_gate))
    grad_up = act_grads * jax.nn.silu(gate_part)
    gate_up_low = jnp.concatenate([grad_gate, grad_up], axis=-1).astype(jnp.bfloat16)
    gate_up_wgrads = jnp.einsum(
        "secd,secf->edf", arrived, gate_up_low, preferred_element_type=jnp.float32
    )
    input_rows = jnp.einsum(
        "secf,edf->secd", gate_up_low, w_gate_up, preferred_element_type=jnp.float32
    ).astype(jnp.bfloat16)
    back_rows = lax.all_to_all(
        input_rows.reshape(members, EXP_DEV * capacity, D),
        "expert",
        split_axis=0,
        concat_axis=0,
        tiled=True,
    ).reshape(expert_total * capacity, D)
    moe_input_grad = jnp.sum(
        back_rows[targets].reshape(tok_rows, TOP, D).astype(jnp.float32), axis=1
    )
    chosen_grads = gate_weights * (
        gate_grads - jnp.sum(gate_weights * gate_grads, axis=-1, keepdims=True)
    )
    logit_grads = jnp.sum(one_hot * chosen_grads[:, :, None], axis=1).astype(jnp.bfloat16)
    router_wgrad = jnp.dot(normed_moe.T, logit_grads, preferred_element_type=jnp.float32)
    normed_moe_grad = moe_input_grad + jnp.dot(
        logit_grads, full_router.T, preferred_element_type=jnp.float32
    )
    unused_moe, moe_pull = jax.vjp(rms_scale, after_attn, gain_moe)
    attn_out_grad, moe_gain_grad = moe_pull(normed_moe_grad)
    resid_grad = grad_final + attn_out_grad
    branch_grad = (RESIDUAL * resid_grad).astype(jnp.bfloat16)
    out_wgrad = jnp.dot(mixed_low.T, branch_grad, preferred_element_type=jnp.float32)
    mixed_grad = jnp.dot(branch_grad, full_out.T, preferred_element_type=jnp.float32).astype(
        jnp.bfloat16
    )
    mixed_heads = jnp.moveaxis(mixed_grad.reshape(tok_rows, KV_HEADS, group_size, HEAD_DIM), 1, 0)
    key_back, value_back = (key_heads, value_heads)

    def head_backward(operands):
        query_head, key_head, value_head, out_grad = operands
        probability = head_probs(query_head, key_head)
        value_grad = jnp.einsum(
            "gqk,qgd->kd",
            probability.astype(jnp.bfloat16),
            out_grad,
            preferred_element_type=jnp.float32,
        )
        prob_grad = jnp.einsum(
            "qgd,kd->gqk", out_grad, value_head, preferred_element_type=jnp.float32
        )
        score_grad = (
            probability
            * (prob_grad - jnp.sum(probability * prob_grad, axis=-1, keepdims=True))
            * ATTN_SCALE
        ).astype(jnp.bfloat16)
        query_grad = jnp.einsum(
            "gqk,kd->qgd", score_grad, key_head, preferred_element_type=jnp.float32
        )
        key_grad = jnp.einsum(
            "gqk,qgd->kd", score_grad, query_head, preferred_element_type=jnp.float32
        )
        return (query_grad, key_grad, value_grad)

    query_grads, key_grads, value_grads = lax.map(
        head_backward, (query_heads, key_back, value_back, mixed_heads)
    )
    query_grad = jnp.moveaxis(query_grads, 0, 1).reshape(tok_rows, HEADS * HEAD_DIM)
    pair_grad_seq = jnp.concatenate(
        [
            jnp.moveaxis(key_grads, 0, 1).reshape(seq_length, pair_width),
            jnp.moveaxis(value_grads, 0, 1).reshape(seq_length, pair_width),
        ],
        axis=1,
    )
    pair_grad = lax.psum_scatter(
        pair_grad_seq.astype(jnp.bfloat16), "expert", scatter_dimension=0, tiled=True
    ).astype(jnp.float32)
    query_grad_low = rotate(query_grad, cosine, -sine_table).astype(jnp.bfloat16)
    pair_grad_low = jnp.concatenate(
        [rotate(pair_grad[:, :pair_width], cosine, -sine_table), pair_grad[:, pair_width:]], axis=1
    ).astype(jnp.bfloat16)
    query_wgrad = jnp.dot(normed.T, query_grad_low, preferred_element_type=jnp.float32)
    pair_wgrad = jnp.dot(normed.T, pair_grad_low, preferred_element_type=jnp.float32)
    normed_grad = jnp.dot(
        query_grad_low, full_query.T, preferred_element_type=jnp.float32
    ) + jnp.dot(pair_grad_low, full_pair.T, preferred_element_type=jnp.float32)
    unused_attn, attn_pull = jax.vjp(rms_scale, tokens_f, gain_attn)
    token_norm_grad, attn_gain_grad = attn_pull(normed_grad)
    token_grad = (resid_grad + token_norm_grad).astype(jnp.bfloat16)
    shared = (
        lax.psum_scatter(query_wgrad, ("dp", "expert"), scatter_dimension=0, tiled=True),
        lax.psum_scatter(pair_wgrad, ("dp", "expert"), scatter_dimension=0, tiled=True),
        lax.psum_scatter(out_wgrad, ("dp", "expert"), scatter_dimension=1, tiled=True),
        lax.psum_scatter(router_wgrad, ("dp", "expert"), scatter_dimension=0, tiled=True),
        lax.psum_scatter(attn_gain_grad, ("dp", "expert"), scatter_dimension=0, tiled=True),
        lax.psum_scatter(moe_gain_grad, ("dp", "expert"), scatter_dimension=0, tiled=True),
    )
    gate_up_share, down_share = (
        lax.psum_scatter(
            gate_up_wgrads.astype(jnp.bfloat16), "dp", scatter_dimension=1, tiled=True
        ).astype(jnp.float32),
        lax.psum_scatter(
            down_wgrads.astype(jnp.bfloat16), "dp", scatter_dimension=2, tiled=True
        ).astype(jnp.float32),
    )
    return (
        result,
        token_grad,
        shared[0],
        shared[1],
        shared[2],
        shared[3],
        shared[4],
        shared[5],
        gate_up_share,
        down_share,
    )


def solution(mesh):
    in_specs = (
        P(("dp", "expert"), None),
        P("dp"),
        P(("dp", "expert"), None),
        P(("dp", "expert"), None),
        P(("dp", "expert"), None),
        P(None, ("dp", "expert")),
        P(("dp", "expert"), None),
        P(("dp", "expert")),
        P(("dp", "expert")),
        P("expert", None, None),
        P("expert", None, None),
        P(("dp", "expert"), None),
    )
    out_specs = (
        P(("dp", "expert"), None),
        P(("dp", "expert"), None),
        P(("dp", "expert"), None),
        P(("dp", "expert"), None),
        P(None, ("dp", "expert")),
        P(("dp", "expert"), None),
        P(("dp", "expert")),
        P(("dp", "expert")),
        P("expert", "dp", None),
        P("expert", None, "dp"),
    )
    return jax.shard_map(shards, mesh=mesh, in_specs=in_specs, out_specs=out_specs, check_vma=False)
```

profile of v0, /device:TPU:0, one launch (start us, length us, event | category | flops | bytes accessed | tf_op | source)
XLA Modules:
  0.0 1843.8 jit_solution(649643439071911868)
XLA Ops:
  10.4 42.1 %all-reduce.5 = (bf16[1536]{0:T(1024)(128)(2,1)S(1)}, bf16[1536]{0:T(1024)(128)(2,1)S(1)}) all-reduce(bf16[1536]{0:T(1024)(128)(2,1)S(1)} %dynamic-update-slice, bf16[1536]{0:T(1024)(128)(2,1)S(1)} %dynamic-update-slice.1), channel_id=1, replica_groups=mesh['dp'=4,'expert'=8] {'dp','expert'}, use_global_device_ids=true, to_apply=%add | all-reduce | flops 3072 | bytes 12288
  54.8 17.8 all-gather.6.cloned.1.call-done
  96.7 41.3 %all-gather.10.cloned.1.call-done = bf16[1536,1536]{1,0:T(8,128)(2,1)} async-done(((bf16[48,1536]{1,0:T(8,128)(2,1)}), bf16[1536,1536]{1,0:T(8,128)(2,1)}) %all-gather.10.cloned.1.call-update) | async-done | bytes 4718608 | tf_op jit(solution)/shard_map/all_gather | solution.py:81
  143.9 32.2 %all-gather.8.cloned.1.call-done = bf16[2048,1024]{1,0:T(8,128)(2,1)} async-done(((bf16[256,1024]{1,0:T(8,128)(2,1)}), bf16[2048,1024]{1,0:T(8,128)(2,1)}) %all-gather.8.cloned.1.call-update) | async-done | bytes 4194320 | tf_op jit(solution)/shard_map/all_gather | solution.py:114
  188.5 100.8 %while.28 = (s32[]{:T(128)}, bf16[8,256,3,64]{1,3,2,0:T(8,128)(2,1)}, bf16[8,2048,64]{1,2,0:T(8,128)(2,1)}, bf16[8,2048,64]{1,2,0:T(8,128)(2,1)}, bf16[8,256,3,6...) while((s32[]{:T(128)}, ...), condition=%wide.region_4.5_spmd.clone.clone, body=%wide.region_1.4_spmd.clone.sunk.clone | while | flops 413665280 | bytes 14477405 | solution.py:137
  295.9 15.1 scatter_custom_fusion
  316.0 120.6 %all-gather = bf16[32,48,16]{1,2,0:T(8,128)(2,1)S(1)} all-gather(bf16[1,48,16]{1,2,0:T(8,128)(2,1)S(1)} %bitcast.376), channel_id=1, replica_groups=mesh['dp'=4,'expert'=8] {'dp','expert'}, dimensions={0}, use_global_device_ids=true | all-gather | bytes 50688 | tf_op jit(solution)/shard_map/all_gather | solution.py:84
  441.1 15.8 scatter_custom_fusion.1
  461.9 14.9 fusion.142
  476.8 73.5 %all-to-all-done.2 = bf16[8,320,1536]{2,1,0:T(8,128)(2,1)} async-done(((bf16[8,320,1536]{2,1,0:T(8,128)(2,1)}), bf16[8,320,1536]{2,1,0:T(8,128)(2,1)}, u32[]{:S(2)}, u32[]{:S(2)}) %all-to-all-start.2) | async-done | bytes 7864352 | tf_op jit(solution)/shard_map/all_to_all | solution.py:192
  583.1 13.7 convert_bitcast_fusion
  603.9 67.7 %all-to-all-done.1 = bf16[8,320,1536]{2,1,0:T(8,128)(2,1)} async-done(((bf16[8,320,1536]{2,1,0:T(8,128)(2,1)}), bf16[8,320,1536]{2,1,0:T(8,128)(2,1)}, u32[]{:S(2)}, u32[]{:S(2)}) %all-to-all-start.1) | async-done | bytes 7864352 | tf_op jit(solution)/shard_map/all_to_all | solution.py:169
  677.1 17.5 gather_fusion
  704.3 61.0 %all-to-all-done.3 = bf16[8,320,1536]{2,1,0:T(8,128)(2,1)} async-done(((bf16[8,320,1536]{2,1,0:T(8,128)(2,1)}), bf16[8,320,1536]{2,1,0:T(8,128)(2,1)}, u32[]{:S(2)}, u32[]{:S(2)}) %all-to-all-start.3) | async-done | bytes 7864352 | tf_op jit(solution)/shard_map/all_to_all | solution.py:211
  765.3 17.5 gather_fusion.1
  794.7 307.4 %while.29 = (s32[]{:T(128)}, f32[8,256,3,64]{1,3,2,0:T(8,128)}, bf16[8,2048,64]{1,2,0:T(8,128)(2,1)}, bf16[8,2048,64]{1,2,0:T(8,128)(2,1)}, bf16[8,2048,64]{1,2,...) while((s32[]{:T(128)}, f32[8,256,3,64]{1,3,2,0:T(8,128)}, ...), condition=%wide.region_24.25_spmd.clone.clone, body=%wide.region_20.24_spmd.clone.sunk.clone | while | flops 1039670784 | bytes 72726648 | solution.py:265
  1130.3 14.0 bitcast_convert_fusion
  1163.4 54.6 %reduce-scatter.24.cloned.1.call-done = bf16[384,1024]{1,0:T(8,128)(2,1)} async-done(((bf16[1536,1024]{1,0:T(8,128)(2,1)}), bf16[384,1024]{1,0:T(8,128)(2,1)}) %reduce-scatter.24.cloned.1.call-update) | async-done | bytes 786448
  1227.5 92.0 %reduce-scatter.22.cloned.1.call-done = f32[48,16]{1,0:T(8,128)} async-done(((f32[1536,16]{1,0:T(8,128)}), f32[48,16]{1,0:T(8,128)}) %reduce-scatter.22.cloned.1.call-update) | async-done | bytes 3088
  1320.9 110.8 %reduce-scatter.20.cloned.1.call-done = bf16[2,384,1024]{2,1,0:T(8,128)(2,1)} async-done(((bf16[2,1536,1024]{2,1,0:T(8,128)(2,1)}), bf16[2,384,1024]{2,1,0:T(8,128)(2,1)}) %reduce-scatter.20.cloned.1.call-update) | async-done | bytes 1572880 | tf_op jit(solution)/shard_map/reduce_scatter | solution.py:300
  1440.0 40.9 %all-reduce.4 = (f32[1536]{0:T(1024)S(1)}, f32[1536]{0:T(1024)S(1)}) all-reduce(f32[1536]{0:T(1024)S(1)} %get-tuple-element.153, f32[1536]{0:T(1024)S(1)} %copy-done.25), channel_id=7, replica_groups=mesh['dp'=4,'expert'=8] {'dp','expert'}, use_global_device_ids=true, to_apply=%region_32.33.clone | all-reduce | flops 3072 | bytes 24576
  1485.6 89.8 %reduce-scatter.18.cloned.1.call-done = f32[1536,48]{0,1:T(8,128)} async-done(((f32[1536,1536]{0,1:T(8,128)}), f32[1536,48]{0,1:T(8,128)}) %reduce-scatter.18.cloned.1.call-update) | async-done | bytes 294928 | tf_op jit(solution)/shard_map/reduce_scatter | solution.py:294
  1575.3 140.8 %reduce-scatter.14.cloned.1.call-done = f32[48,1536]{1,0:T(8,128)} async-done(((f32[1536,1536]{1,0:T(8,128)}), f32[48,1536]{1,0:T(8,128)}) %reduce-scatter.14.cloned.1.call-update) | async-done | bytes 294928 | tf_op jit(solution)/shard_map/reduce_scatter | solution.py:292
  1716.2 120.9 %reduce-scatter.16.cloned.1.call-done = f32[48,1024]{1,0:T(8,128)} async-done(((f32[1536,1024]{1,0:T(8,128)}), f32[48,1024]{1,0:T(8,128)}) %reduce-scatter.16.cloned.1.call-update) | async-done | bytes 196624 | tf_op jit(solution)/shard_map/reduce_scatter | solution.py:293
  (271 shorter events, 614.2 us)
Async XLA Ops:
  7.2 543.1 %copy-start = (bf16[2,512,1536]{2,1,0:T(8,128)(2,1)S(1)}, bf16[2,512,1536]{2,1,0:T(8,128)(2,1)}, u32[]{:S(2)}) copy-start(bf16[2,512,1536]{2,1,0:T(8,128)(2,1)} %param.26) | copy-start | bytes 9437188
  7.2 65.4 %all-gather.6.cloned.1.call-start = ((), (), s32[]{:S(2)}) async-start(), calls=%async_computation.11 | async-start | bytes 3244032 | tf_op jit(solution)/shard_map/all_gather | solution.py:82
  7.9 130.1 %all-gather.10.cloned.1.call-start = ((), (), s32[]{:S(2)}) async-start(), calls=%async_computation.13 | async-start | bytes 4866048 | tf_op jit(solution)/shard_map/all_gather | solution.py:81
  8.7 167.4 %all-gather.8.cloned.1.call-start = ((), (), s32[]{:S(2)}) async-start(), calls=%async_computation.12 | async-start | bytes 4718592 | tf_op jit(solution)/shard_map/all_gather | solution.py:114
  52.5 85.5 %copy-start.18 = (f32[1536]{0:T(1024)}, f32[1536]{0:T(1024)S(1)}, u32[]{:S(2)}) copy-start(f32[1536]{0:T(1024)S(1)} %convert_element_type.126) | copy-start | bytes 18436
  53.9 21.8 %copy-start.26 = (f32[256]{0:T(256)}, f32[256]{0:T(256)S(1)}, u32[]{:S(2)}) copy-start(f32[256]{0:T(256)S(1)} %fusion.157) | copy-start | bytes 3076
  53.9 84.1 %copy-start.23 = (f32[256]{0:T(256)}, f32[256]{0:T(256)S(1)}, u32[]{:S(2)}) copy-start(f32[256]{0:T(256)S(1)} %fusion.172) | copy-start | bytes 3076
  54.8 87.9 %copy-start.15 = (f32[256,32]{0,1:T(8,128)}, f32[256,32]{0,1:T(8,128)S(1)}, u32[]{:S(2)}) copy-start(f32[256,32]{0,1:T(8,128)S(1)} %get-tuple-element.224) | copy-start | bytes 98308
  79.4 16.2 copy-start.14
  83.3 206.0 %all-gather.12.cloned.1.call-start = ((), (), s32[]{:S(2)}) async-start(), calls=%async_computation.14 | async-start | bytes 4866048 | tf_op jit(solution)/shard_map/all_gather | solution.py:83
  311.0 146.0 %all-to-all-start = ((bf16[8,320,1536]{2,1,0:T(8,128)(2,1)}), bf16[8,320,1536]{2,1,0:T(8,128)(2,1)}, u32[]{:S(2)}, u32[]{:S(2)}) async-start(bf16[8,320,1536]{2,1,0:T(8,128)(2,1)} %bitcast.347), calls=%async_computation | async-start | bytes 15728640 | tf_op jit(solution)/shard_map/all_to_all | solution.py:159
  457.0 93.3 %all-to-all-start.2 = ((bf16[8,320,1536]{2,1,0:T(8,128)(2,1)}), bf16[8,320,1536]{2,1,0:T(8,128)(2,1)}, u32[]{:S(2)}, u32[]{:S(2)}) async-start(bf16[8,320,1536]{2,1,0:T(8,128)(2,1)} %bitcast.348), calls=%async_computation.2 | async-start | bytes 15728640 | tf_op jit(solution)/shard_map/all_to_all | solution.py:192
  578.0 93.6 %all-to-all-start.1 = ((bf16[8,320,1536]{2,1,0:T(8,128)(2,1)}), bf16[8,320,1536]{2,1,0:T(8,128)(2,1)}, u32[]{:S(2)}, u32[]{:S(2)}) async-start(bf16[8,320,1536]{2,1,0:T(8,128)(2,1)} %bitcast.349), calls=%async_computation.1 | async-start | bytes 15728640 | tf_op jit(solution)/shard_map/all_to_all | solution.py:169
  671.6 93.7 %all-to-all-start.3 = ((bf16[8,320,1536]{2,1,0:T(8,128)(2,1)}), bf16[8,320,1536]{2,1,0:T(8,128)(2,1)}, u32[]{:S(2)}, u32[]{:S(2)}) async-start(bf16[8,320,1536]{2,1,0:T(8,128)(2,1)} %bitcast.346), calls=%async_computation.3 | async-start | bytes 15728640 | tf_op jit(solution)/shard_map/all_to_all | solution.py:211
  676.8 481.4 %reduce-scatter.12.cloned.1.call-start = ((), (), s32[]{:S(2)}) async-start(), calls=%async_computation.15 | async-start | bytes 4718592 | tf_op jit(solution)/shard_map/reduce_scatter | solution.py:276
  704.3 85.6 %copy-start.21 = (bf16[256,16]{0,1:T(8,128)(2,1)}, bf16[256,16]{0,1:T(8,128)(2,1)S(1)}, u32[]{:S(2)}) copy-start(bf16[256,16]{0,1:T(8,128)(2,1)S(1)} %select_reduce_fusion) | copy-start | bytes 24580
  1107.0 111.0 %reduce-scatter.24.cloned.1.call-start = ((), (), s32[]{:S(2)}) async-start(), calls=%async_computation.21 | async-start | bytes 3932160
  1127.8 191.7 %reduce-scatter.22.cloned.1.call-start = ((), (), s32[]{:S(2)}) async-start(), calls=%async_computation.20 | async-start | bytes 811008
  1130.3 301.4 %reduce-scatter.20.cloned.1.call-start = ((), (), s32[]{:S(2)}) async-start(), calls=%async_computation.19 | async-start | bytes 7864320 | tf_op jit(solution)/shard_map/reduce_scatter | solution.py:300
  1144.4 431.0 %reduce-scatter.18.cloned.1.call-start = ((), (), s32[]{:S(2)}) async-start(), calls=%async_computation.18 | async-start | bytes 9732096 | tf_op jit(solution)/shard_map/reduce_scatter | solution.py:294
  1151.1 565.1 %reduce-scatter.14.cloned.1.call-start = ((), (), s32[]{:S(2)}) async-start(), calls=%async_computation.16 | async-start | bytes 9732096 | tf_op jit(solution)/shard_map/reduce_scatter | solution.py:292
  1158.0 679.0 %reduce-scatter.16.cloned.1.call-start = ((), (), s32[]{:S(2)}) async-start(), calls=%async_computation.17 | async-start | bytes 6488064 | tf_op jit(solution)/shard_map/reduce_scatter | solution.py:293
  1435.3 46.8 %copy-start.27 = (f32[256]{0:T(256)S(1)}, f32[256]{0:T(256)}, u32[]{:S(2)}) copy-start(f32[256]{0:T(256)} %copy-done.26) | copy-start | bytes 3076
  1435.3 401.7 %copy-start.1 = (bf16[2,512,1536]{2,1,0:T(8,128)(2,1)S(1)}, bf16[2,512,1536]{2,1,0:T(8,128)(2,1)}, u32[]{:S(2)}) copy-start(bf16[2,512,1536]{2,1,0:T(8,128)(2,1)} %param.26) | copy-start | bytes 9437188
  (26 other events, 79.7 us)
Sparse Core Ops, SparseCore 0:
  10.9 61.6 all-gather.5
  75.5 62.4 all-gather.9
  140.5 35.5 all-gather.7
  178.8 63.6 all-gather.11
  1107.2 47.6 reduce-scatter.11
  1157.7 60.2 reduce-scatter.23
  1223.9 95.5 reduce-scatter.21
  1321.9 109.8 reduce-scatter.19
  1439.2 136.1 reduce-scatter.17
  1581.7 134.4 reduce-scatter.13
  1723.3 113.6 reduce-scatter.15
where the time goes:
time: 1850 us; the launch traced here: 1840 us
  waiting for transfers between devices  904 us (49%)
  matrix products  491 us (27%)
  blocking collectives  204 us (11%)
  local copies, waits for them, and re-layouts  109 us (6%)
  other arithmetic  98.9 us (5%)
  starting transfers between devices  21.5 us (1%)
    unnamed x13, waiting for transfers between devices  148 us
    reduce_scatter x1, waiting for transfers between devices, shards(): lax.psum_scatter(query_wgrad, ('dp', 'expert'), scatter_dimension=0, tile...  141 us
    reduce_scatter x1, waiting for transfers between devices, shards(): lax.psum_scatter(pair_wgrad, ('dp', 'expert'), scatter_dimension=0, tiled...  121 us
    all_gather x1, blocking collectives, shards(): lax.all_gather(w_router, ('dp', 'expert'), axis=0, tiled=True)  121 us
    reduce_scatter x1, waiting for transfers between devices, shards(): lax.psum_scatter(gate_up_wgrads.astype(jnp.bfloat16), 'dp', scatter_dimen...  111 us
    sub x16, matrix products, head_probs(): exponent = jnp.exp(scores - largest)  95.9 us
    reduce_scatter x1, waiting for transfers between devices, shards(): lax.psum_scatter(out_wgrad, ('dp', 'expert'), scatter_dimension=1, tiled=...  89.8 us
    dot_general x8, matrix products, head_backward(): jnp.einsum('gqk,kd->qgd', score_grad, key_head, preferred_element_type=jn...  87.6 us
  transfers between devices with their start and end apart: 15, of which 12 were waited for; matrix products, arithmetic and copies ran while one was open for 16% of the time, Pallas kernels for 0%

commit v1 on v0

--- a/solution.py
+++ b/solution.py
@@ -1,3 +1,4 @@
+import functools
 import jax
 import jax.numpy as jnp
 from jax import lax
@@ -16,6 +17,39 @@
 EPSILON = 1e-06
 ROPE_BASE = 10000.0
 MASKED = -1e30
+
+
+def _meet_hubs(arr, out_dim, panel):
+    answer = arr.shape
+    x_now = arr.reshape(*answer[:out_dim], panel, answer[out_dim] // panel, *answer[out_dim + 1 :])
+    return jnp.moveaxis(x_now, out_dim, 0)
+
+
+def lift_wires(local, pos_dim):
+    local = jnp.moveaxis(local, 0, pos_dim)
+    step_out = local.shape
+    return local.reshape(
+        *step_out[:pos_dim], step_out[pos_dim] * step_out[pos_dim + 1], *step_out[pos_dim + 2 :]
+    )
+
+
+def wait_node(own_rows, axis_key, a0, local_array):
+    v_now = jax.lax.axis_size(axis_key)
+    earlier = jax.lax.axis_index(axis_key)
+    carry_out, prior = (v_now, earlier)
+    current_arr = _meet_hubs(own_rows, a0, carry_out)
+    history = [current_arr[prior]]
+    for num in [*range(1, carry_out)]:
+        current_value = current_arr[prior ^ num]
+        local_out = jax.lax.ppermute(
+            current_value, axis_key, [(dev_j, dev_j ^ num) for dev_j in range(carry_out)]
+        )
+        history.append(local_out)
+    current_arr = jnp.stack(history)[prior ^ jnp.arange(carry_out)]
+    return lift_wires(current_arr, local_array)
+
+
+produce_files = functools.partial(wait_node, axis_key="expert", a0=0, local_array=0)
 
 
 def rms_scale(values, gain_vec):
@@ -166,13 +200,9 @@
     expert_out = jnp.einsum(
         "secf,efd->secd", activated, w_down, preferred_element_type=jnp.float32
     ).astype(jnp.bfloat16)
-    replies = lax.all_to_all(
-        expert_out.reshape(members, EXP_DEV * capacity, D),
-        "expert",
-        split_axis=0,
-        concat_axis=0,
-        tiled=True,
-    ).reshape(expert_total * capacity, D)
+    replies = produce_files(expert_out.reshape(members, EXP_DEV * capacity, D)).reshape(
+        expert_total * capacity, D
+    )
     returned_f = replies[targets].reshape(tok_rows, TOP, D).astype(jnp.float32)
     combined = jnp.sum(gate_weights[:, :, None] * returned_f, axis=1)
     result = (after_attn + RESIDUAL * combined).astype(jnp.bfloat16)

time: 1850 us -> 1890 us (1.022)
  local copies, waits for them, and re-layouts: 109 us -> 132 us
    ppermute x0 -> x7, waiting for transfers between devices: none -> 137 us  [wait_node(): jax.lax.ppermute(current_value, axis_key, [(dev_j, dev_j ^ num) for dev_j...]
    all_to_all x1 -> x0, waiting for transfers between devices: 67.7 us -> none  [shards(): lax.all_to_all(expert_out.reshape(members, EXP_DEV * capacity, D), 'exper...]
    all_to_all x1, waiting for transfers between devices: 61 us -> 0.01 us  [shards(): lax.all_to_all(input_rows.reshape(members, EXP_DEV * capacity, D), 'exper...]
  transfers between devices with their start and end apart: 15 -> 21, of which waited for: 12 -> 13; matrix products, arithmetic and copies ran while one was open for 16% -> 17% of each run, Pallas kernels for 0% -> 0%
where the time goes in v1:
time: 1890 us; the launch traced here: 1880 us
  waiting for transfers between devices  916 us (48%)
  matrix products  494 us (26%)
  blocking collectives  204 us (11%)
  local copies, waits for them, and re-layouts  132 us (7%)
  other arithmetic  97.5 us (5%)
  starting transfers between devices  23.9 us (1%)
    unnamed x13, waiting for transfers between devices  158 us
    reduce_scatter x1, waiting for transfers between devices, shards(): lax.psum_scatter(query_wgrad, ('dp', 'expert'), scatter_dimension=0, tile...  141 us
    ppermute x7, waiting for transfers between devices, wait_node(): jax.lax.ppermute(current_value, axis_key, [(dev_j, dev_j ^ num) for dev_j...  137 us
    reduce_scatter x1, waiting for transfers between devices, shards(): lax.psum_scatter(pair_wgrad, ('dp', 'expert'), scatter_dimension=0, tiled...  121 us
    all_gather x1, blocking collectives, shards(): lax.all_gather(w_router, ('dp', 'expert'), axis=0, tiled=True)  121 us
    reduce_scatter x1, waiting for transfers between devices, shards(): lax.psum_scatter(gate_up_wgrads.astype(jnp.bfloat16), 'dp', scatter_dimen...  104 us
    sub x16, matrix products, head_probs(): exponent = jnp.exp(scores - largest)  95.5 us
    reduce_scatter x1, waiting for transfers between devices, shards(): lax.psum_scatter(out_wgrad, ('dp', 'expert'), scatter_dimension=1, tiled=...  89.3 us
  transfers between devices with their start and end apart: 21, of which 13 were waited for; matrix products, arithmetic and copies ran while one was open for 17% of the time, Pallas kernels for 0%

profile of v1, /device:TPU:0, one launch (start us, length us, event | category | flops | bytes accessed | tf_op | source)
XLA Modules:
  0.0 1882.8 jit_solution(4268014009549977786)
XLA Ops:
  10.4 42.1 %all-reduce.5 = (bf16[1536]{0:T(1024)(128)(2,1)S(1)}, bf16[1536]{0:T(1024)(128)(2,1)S(1)}) all-reduce(bf16[1536]{0:T(1024)(128)(2,1)S(1)} %dynamic-update-slice, bf16[1536]{0:T(1024)(128)(2,1)S(1)} %dynamic-update-slice.1), channel_id=1, replica_groups=mesh['dp'=4,'expert'=8] {'dp','expert'}, use_global_device_ids=true, to_apply=%add | all-reduce | flops 3072 | bytes 12288
  55.3 17.3 all-gather.6.cloned.1.call-done
  95.1 42.9 %all-gather.10.cloned.1.call-done = bf16[1536,1536]{1,0:T(8,128)(2,1)} async-done(((bf16[48,1536]{1,0:T(8,128)(2,1)}), bf16[1536,1536]{1,0:T(8,128)(2,1)}) %all-gather.10.cloned.1.call-update) | async-done | bytes 4718608 | tf_op jit(solution)/shard_map/all_gather | solution.py:115
  143.9 32.2 %all-gather.8.cloned.1.call-done = bf16[2048,1024]{1,0:T(8,128)(2,1)} async-done(((bf16[256,1024]{1,0:T(8,128)(2,1)}), bf16[2048,1024]{1,0:T(8,128)(2,1)}) %all-gather.8.cloned.1.call-update) | async-done | bytes 4194320 | tf_op jit(solution)/shard_map/all_gather | solution.py:148
  188.5 100.7 %while.28 = (s32[]{:T(128)}, bf16[8,256,3,64]{1,3,2,0:T(8,128)(2,1)}, bf16[8,2048,64]{1,2,0:T(8,128)(2,1)}, bf16[8,2048,64]{1,2,0:T(8,128)(2,1)}, bf16[8,256,3,6...) while((s32[]{:T(128)}, ...), condition=%wide.region_4.5_spmd.clone.clone, body=%wide.region_1.4_spmd.clone.sunk.clone | while | flops 413665280 | bytes 14477413 | solution.py:171
  295.8 15.0 scatter_custom_fusion
  315.8 120.7 %all-gather = bf16[32,48,16]{1,2,0:T(8,128)(2,1)S(1)} all-gather(bf16[1,48,16]{1,2,0:T(8,128)(2,1)S(1)} %bitcast.411), channel_id=1, replica_groups=mesh['dp'=4,'expert'=8] {'dp','expert'}, dimensions={0}, use_global_device_ids=true | all-gather | bytes 50688 | tf_op jit(solution)/shard_map/all_gather | solution.py:118
  441.1 15.8 scatter_custom_fusion.1
  461.8 15.0 fusion.142
  476.8 73.4 %all-to-all-done.1 = bf16[8,320,1536]{2,1,0:T(8,128)(2,1)} async-done(((bf16[8,320,1536]{2,1,0:T(8,128)(2,1)}), bf16[8,320,1536]{2,1,0:T(8,128)(2,1)}, u32[]{:S(2)}, u32[]{:S(2)}) %all-to-all-start.1) | async-done | bytes 7864352 | tf_op jit(solution)/shard_map/all_to_all | solution.py:222
  564.6 13.7 convert_bitcast_fusion
  621.0 78.3 %collective-permute-done.1 = bf16[1,320,1536]{2,1,0:T(8,128)(2,1)} collective-permute-done((bf16[1,320,1536]{2,1,0:T(8,128)(2,1)}, bf16[1,320,1536]{2,1,0:T(8,128)(2,1)}, u32[]{:S(2)}, u32[]{:S(2)}) %collective-permute-start.1) | collective-permute-done | bytes 983072 | tf_op jit(solution)/shard_map/ppermute | solution.py:44
  703.0 58.5 %collective-permute-done.2 = bf16[1,320,1536]{2,1,0:T(8,128)(2,1)S(1)} collective-permute-done((bf16[1,320,1536]{2,1,0:T(8,128)(2,1)}, bf16[1,320,1536]{2,1,0:T(8,128)(2,1)S(1)}, u32[]{:S(2)}, u32[]{:S(2)}) %collective-permute-start.2) | collective-permute-done | bytes 983072 | tf_op jit(solution)/shard_map/ppermute | solution.py:44
  774.7 17.6 gather_fusion.1
  801.9 17.7 gather_fusion.2
  833.4 306.4 %while.29 = (s32[]{:T(128)}, f32[8,256,3,64]{1,3,2,0:T(8,128)}, bf16[8,2048,64]{1,2,0:T(8,128)(2,1)}, bf16[8,2048,64]{1,2,0:T(8,128)(2,1)}, bf16[8,2048,64]{1,2,...) while((s32[]{:T(128)}, f32[8,256,3,64]{1,3,2,0:T(8,128)}, ...), condition=%wide.region_24.25_spmd.clone.clone, body=%wide.region_20.24_spmd.clone.sunk.clone | while | flops 1039670784 | bytes 72726648 | solution.py:295
  1166.9 13.9 bitcast_convert_fusion
  1199.7 95.5 %reduce-scatter.22.cloned.1.call-done = f32[48,16]{1,0:T(8,128)} async-done(((f32[1536,16]{1,0:T(8,128)}), f32[48,16]{1,0:T(8,128)}) %reduce-scatter.22.cloned.1.call-update) | async-done | bytes 3088
  1296.6 60.9 %reduce-scatter.24.cloned.1.call-done = bf16[384,1024]{1,0:T(8,128)(2,1)} async-done(((bf16[1536,1024]{1,0:T(8,128)(2,1)}), bf16[384,1024]{1,0:T(8,128)(2,1)}) %reduce-scatter.24.cloned.1.call-update) | async-done | bytes 786448
  1367.0 103.7 %reduce-scatter.20.cloned.1.call-done = bf16[2,384,1024]{2,1,0:T(8,128)(2,1)} async-done(((bf16[2,1536,1024]{2,1,0:T(8,128)(2,1)}), bf16[2,384,1024]{2,1,0:T(8,128)(2,1)}) %reduce-scatter.20.cloned.1.call-update) | async-done | bytes 1572880 | tf_op jit(solution)/shard_map/reduce_scatter | solution.py:330
  1479.4 40.9 %all-reduce.4 = (f32[1536]{0:T(1024)S(1)}, f32[1536]{0:T(1024)S(1)}) all-reduce(f32[1536]{0:T(1024)S(1)} %get-tuple-element.153, f32[1536]{0:T(1024)S(1)} %copy-done.30), channel_id=7, replica_groups=mesh['dp'=4,'expert'=8] {'dp','expert'}, use_global_device_ids=true, to_apply=%region_32.33.clone | all-reduce | flops 3072 | bytes 24576
  1524.9 89.3 %reduce-scatter.18.cloned.1.call-done = f32[1536,48]{0,1:T(8,128)} async-done(((f32[1536,1536]{0,1:T(8,128)}), f32[1536,48]{0,1:T(8,128)}) %reduce-scatter.18.cloned.1.call-update) | async-done | bytes 294928 | tf_op jit(solution)/shard_map/reduce_scatter | solution.py:324
  1614.2 140.9 %reduce-scatter.14.cloned.1.call-done = f32[48,1536]{1,0:T(8,128)} async-done(((f32[1536,1536]{1,0:T(8,128)}), f32[48,1536]{1,0:T(8,128)}) %reduce-scatter.14.cloned.1.call-update) | async-done | bytes 294928 | tf_op jit(solution)/shard_map/reduce_scatter | solution.py:322
  1755.1 120.9 %reduce-scatter.16.cloned.1.call-done = f32[48,1024]{1,0:T(8,128)} async-done(((f32[1536,1024]{1,0:T(8,128)}), f32[48,1024]{1,0:T(8,128)}) %reduce-scatter.16.cloned.1.call-update) | async-done | bytes 196624 | tf_op jit(solution)/shard_map/reduce_scatter | solution.py:323
  (300 shorter events, 641.3 us)
Async XLA Ops:
  7.2 543.0 %copy-start = (bf16[2,512,1536]{2,1,0:T(8,128)(2,1)S(1)}, bf16[2,512,1536]{2,1,0:T(8,128)(2,1)}, u32[]{:S(2)}) copy-start(bf16[2,512,1536]{2,1,0:T(8,128)(2,1)} %param.26) | copy-start | bytes 9437188
  7.2 65.4 %all-gather.6.cloned.1.call-start = ((), (), s32[]{:S(2)}) async-start(), calls=%async_computation.10 | async-start | bytes 3244032 | tf_op jit(solution)/shard_map/all_gather | solution.py:116
  7.9 130.1 %all-gather.10.cloned.1.call-start = ((), (), s32[]{:S(2)}) async-start(), calls=%async_computation.12 | async-start | bytes 4866048 | tf_op jit(solution)/shard_map/all_gather | solution.py:115
  8.7 167.4 %all-gather.8.cloned.1.call-start = ((), (), s32[]{:S(2)}) async-start(), calls=%async_computation.11 | async-start | bytes 4718592 | tf_op jit(solution)/shard_map/all_gather | solution.py:148
  55.3 87.4 %copy-start.18 = (f32[256,32]{0,1:T(8,128)}, f32[256,32]{0,1:T(8,128)S(1)}, u32[]{:S(2)}) copy-start(f32[256,32]{0,1:T(8,128)S(1)} %get-tuple-element.232) | copy-start | bytes 98308
  83.3 205.9 %all-gather.12.cloned.1.call-start = ((), (), s32[]{:S(2)}) async-start(), calls=%async_computation.13 | async-start | bytes 4866048 | tf_op jit(solution)/shard_map/all_gather | solution.py:117
  310.8 146.1 %all-to-all-start = ((bf16[8,320,1536]{2,1,0:T(8,128)(2,1)}), bf16[8,320,1536]{2,1,0:T(8,128)(2,1)}, u32[]{:S(2)}, u32[]{:S(2)}) async-start(bf16[8,320,1536]{2,1,0:T(8,128)(2,1)} %bitcast.382), calls=%async_computation | async-start | bytes 15728640 | tf_op jit(solution)/shard_map/all_to_all | solution.py:193
  456.9 93.4 %all-to-all-start.1 = ((bf16[8,320,1536]{2,1,0:T(8,128)(2,1)}), bf16[8,320,1536]{2,1,0:T(8,128)(2,1)}, u32[]{:S(2)}, u32[]{:S(2)}) async-start(bf16[8,320,1536]{2,1,0:T(8,128)(2,1)} %bitcast.381), calls=%async_computation.1 | async-start | bytes 15728640 | tf_op jit(solution)/shard_map/all_to_all | solution.py:222
  585.3 216.6 %all-to-all-start.2 = ((bf16[8,320,1536]{2,1,0:T(8,128)(2,1)}), bf16[8,320,1536]{2,1,0:T(8,128)(2,1)}, u32[]{:S(2)}, u32[]{:S(2)}) async-start(bf16[8,320,1536]{2,1,0:T(8,128)(2,1)} %bitcast.380), calls=%async_computation.2 | async-start | bytes 15728640 | tf_op jit(solution)/shard_map/all_to_all | solution.py:241
  590.2 604.3 %reduce-scatter.12.cloned.1.call-start = ((), (), s32[]{:S(2)}) async-start(), calls=%async_computation.14 | async-start | bytes 4718592 | tf_op jit(solution)/shard_map/reduce_scatter | solution.py:306
  612.1 6.2 collective-permute-start
  612.5 86.9 %collective-permute-start.1 = (bf16[1,320,1536]{2,1,0:T(8,128)(2,1)}, bf16[1,320,1536]{2,1,0:T(8,128)(2,1)}, u32[]{:S(2)}, u32[]{:S(2)}) collective-permute-start(bf16[1,320,1536]{2,1,0:T(8,128)(2,1)} %get-tuple-element.213), channel_id=1, source_target_pairs={{0,2},{1,3},{2,0},{3,1},{4,6},{5,7},{6,4},{7,5},{8,10},{9,11},{10,... | collective-permute-start | bytes 2949128 | tf_op jit(solution)/shard_map/ppermute | solution.py:44
  614.4 151.6 %collective-permute-start.6 = (bf16[1,320,1536]{2,1,0:T(8,128)(2,1)}, bf16[1,320,1536]{2,1,0:T(8,128)(2,1)S(1)}, u32[]{:S(2)}, u32[]{:S(2)}) collective-permute-start(bf16[1,320,1536]{2,1,0:T(8,128)(2,1)} %get-tuple-element.208), channel_id=1, source_target_pairs={{0,7},{1,6},{2,5},{3,4},{4,3},{5,2},{6,1},{7,0},{8,15},{9,14},{10,... | collective-permute-start | bytes 2949128 | tf_op jit(solution)/shard_map/ppermute | solution.py:44
  615.6 149.3 %collective-permute-start.5 = (bf16[1,320,1536]{2,1,0:T(8,128)(2,1)}, bf16[1,320,1536]{2,1,0:T(8,128)(2,1)S(1)}, u32[]{:S(2)}, u32[]{:S(2)}) collective-permute-start(bf16[1,320,1536]{2,1,0:T(8,128)(2,1)} %get-tuple-element.209), channel_id=1, source_target_pairs={{0,6},{1,7},{2,4},{3,5},{4,2},{5,3},{6,0},{7,1},{8,14},{9,15},{10,... | collective-permute-start | bytes 2949128 | tf_op jit(solution)/shard_map/ppermute | solution.py:44
  617.1 146.8 %collective-permute-start.4 = (bf16[1,320,1536]{2,1,0:T(8,128)(2,1)}, bf16[1,320,1536]{2,1,0:T(8,128)(2,1)S(1)}, u32[]{:S(2)}, u32[]{:S(2)}) collective-permute-start(bf16[1,320,1536]{2,1,0:T(8,128)(2,1)} %get-tuple-element.210), channel_id=1, source_target_pairs={{0,5},{1,4},{2,7},{3,6},{4,1},{5,0},{6,3},{7,2},{8,13},{9,12},{10,... | collective-permute-start | bytes 2949128 | tf_op jit(solution)/shard_map/ppermute | solution.py:44
  618.3 143.2 %collective-permute-start.2 = (bf16[1,320,1536]{2,1,0:T(8,128)(2,1)}, bf16[1,320,1536]{2,1,0:T(8,128)(2,1)S(1)}, u32[]{:S(2)}, u32[]{:S(2)}) collective-permute-start(bf16[1,320,1536]{2,1,0:T(8,128)(2,1)} %get-tuple-element.212), channel_id=1, source_target_pairs={{0,3},{1,2},{2,1},{3,0},{4,7},{5,6},{6,5},{7,4},{8,11},{9,10},{10,... | collective-permute-start | bytes 2949128 | tf_op jit(solution)/shard_map/ppermute | solution.py:44
  699.3 63.5 %collective-permute-start.3 = (bf16[1,320,1536]{2,1,0:T(8,128)(2,1)}, bf16[1,320,1536]{2,1,0:T(8,128)(2,1)S(1)}, u32[]{:S(2)}, u32[]{:S(2)}) collective-permute-start(bf16[1,320,1536]{2,1,0:T(8,128)(2,1)} %get-tuple-element.211), channel_id=1, source_target_pairs={{0,4},{1,5},{2,6},{3,7},{4,0},{5,1},{6,2},{7,3},{8,12},{9,13},{10,... | collective-permute-start | bytes 2949128 | tf_op jit(solution)/shard_map/ppermute | solution.py:44
  1144.7 150.5 %reduce-scatter.22.cloned.1.call-start = ((), (), s32[]{:S(2)}) async-start(), calls=%async_computation.19 | async-start | bytes 811008
  1146.1 211.4 %reduce-scatter.24.cloned.1.call-start = ((), (), s32[]{:S(2)}) async-start(), calls=%async_computation.20 | async-start | bytes 3932160
  1166.9 303.8 %reduce-scatter.20.cloned.1.call-start = ((), (), s32[]{:S(2)}) async-start(), calls=%async_computation.18 | async-start | bytes 7864320 | tf_op jit(solution)/shard_map/reduce_scatter | solution.py:330
  1180.9 433.3 %reduce-scatter.18.cloned.1.call-start = ((), (), s32[]{:S(2)}) async-start(), calls=%async_computation.17 | async-start | bytes 9732096 | tf_op jit(solution)/shard_map/reduce_scatter | solution.py:324
  1187.6 567.5 %reduce-scatter.14.cloned.1.call-start = ((), (), s32[]{:S(2)}) async-start(), calls=%async_computation.15 | async-start | bytes 9732096 | tf_op jit(solution)/shard_map/reduce_scatter | solution.py:322
  1194.5 681.5 %reduce-scatter.16.cloned.1.call-start = ((), (), s32[]{:S(2)}) async-start(), calls=%async_computation.16 | async-start | bytes 6488064 | tf_op jit(solution)/shard_map/reduce_scatter | solution.py:323
  1470.7 405.3 %copy-start.1 = (bf16[2,512,1536]{2,1,0:T(8,128)(2,1)S(1)}, bf16[2,512,1536]{2,1,0:T(8,128)(2,1)}, u32[]{:S(2)}) copy-start(bf16[2,512,1536]{2,1,0:T(8,128)(2,1)} %param.26) | copy-start | bytes 9437188
  (35 other events, 390.0 us)
Sparse Core Ops, SparseCore 0:
  10.9 61.6 all-gather.5
  75.5 62.4 all-gather.9
  140.5 35.5 all-gather.7
  178.8 63.6 all-gather.11
  1144.8 48.4 reduce-scatter.11
  1199.6 95.4 reduce-scatter.21
  1298.1 59.3 reduce-scatter.23
  1359.9 110.7 reduce-scatter.19
  1478.2 135.9 reduce-scatter.17
  1620.5 134.5 reduce-scatter.13
  1762.3 113.6 reduce-scatter.15
